TPU v7x, 32 devices: a whole 2x2x4 slice. The times are simulated.
32 devices in a mesh: groups: 2 (over x), roll: 4 (over y, core), rows: 4 (over z).
Axes of the slice: x: 2, y: 2, z: 4, core: 2. Of those that a mesh axis runs over, the one named last changes fastest.
Arguments:
- latent_slabs: bfloat16 [16, 3, 32, 8, 16], P(('groups', 'roll'), None, 'rows'), parts along dimension 0, may hold values from -18 to 18, as said below
- prior_latents: bfloat16 [16, 2, 32, 8, 16], P(('groups', 'roll'), None, 'rows'), parts along dimension 0, may hold values from -6 to 6
- prior_features: bfloat16 [16, 2, 32, 8, 512], P(('groups', 'roll'), None, 'rows'), parts along dimension 0, may hold values from -6 to 6
- lengths: int32 [16], P(('groups', 'roll')), parts along dimension 0, may hold values from 1 to 3
- starts: int32 [16], P(('groups', 'roll')), parts along dimension 0, may hold values from 0 to 6, as said below
- move_plan: int32 [16], P(('groups', 'roll')), parts along dimension 0, may hold values from -1 to 3, as said below
- entry_weight: bfloat16 [432, 512], replicated, may hold values from -0.3125 to 0.3125
- block_weight: bfloat16 [13824, 512], P(None, ('roll', 'rows')), may hold values from -0.0546875 to 0.0546875
- norm_gain: float32 [512], replicated, may hold values from 0.25 to 1.75
- norm_shift: float32 [512], replicated, may hold values from -1.2 to 1.2
Outputs:
- decoded: bfloat16 [16, 3, 32, 8, 512], P(('groups', 'roll'), None, 'rows'), parts along dimension 0
There are 2 independent parts, one for each index of `groups`. A program takes and returns all parts, laid end to end along the dimension named above; an argument that names none is the same for every part. Nothing has to cross between parts.
Inputs may be any that keep to these rules, and one draw needn't show every extreme that they name: `latent_slabs`: normal or uniform values times a scale that varies over the rows. `starts`: multiples of 3. `move_plan`: A value d * 1 + c names compute slot c of roll index d. Every compute slot of the part is named by exactly one slab, and the slabs held by one roll index name at most 1 slots of any one roll index.
All inputs are finite; a program needn't handle non-finite values.
Results may differ from a plain program's by a relative error of at most 0.0023.
Values may be sent and summed in bfloat16 or wider, within the bound.
A program may use at most 128 MiB of HBM per device.

v0:
```python
import jax
import jax.numpy as jnp
from jax import lax
from jax.sharding import PartitionSpec as P

GROUPS = 32


EPSILON = 1e-06


def padded(x, sides, width):
    for axis, dim in sides:
        count, length = (lax.axis_size(axis), x.shape[dim])
        up = [(i, (i + 1) % count) for i in range(count - 1)]
        down = [(j, i) for i, j in up]
        last = lax.slice_in_dim(x, length - width, length, axis=dim)
        first = lax.slice_in_dim(x, 0, width, axis=dim)
        before = lax.ppermute(last, axis, up)
        after = lax.ppermute(first, axis, down)
        x = jnp.concatenate([before, x, after], axis=dim)
    return x


def column_pad(extended):
    return jnp.pad(extended, ((0, 0), (0, 0), (0, 0), (1, 1), (0, 0)))


def convolve(extended, weights):
    slots = extended.shape[0]
    frames = extended.shape[1] - 2
    height = extended.shape[2] - 2
    widths = extended.shape[3] - 2
    channels = extended.shape[4]
    accumulated = jnp.zeros((slots * frames * height * widths, weights.shape[1]), jnp.float32)
    for tap_index in range(27):
        step_t = tap_index // 9
        step_h = tap_index // 3 % 3
        step_w = tap_index % 3
        window = extended[
            :, step_t : step_t + frames, step_h : step_h + height, step_w : step_w + widths, :
        ]
        accumulated = accumulated + jnp.dot(
            window.reshape(-1, channels),
            weights[tap_index * channels : (tap_index + 1) * channels],
            preferred_element_type=jnp.float32,
        )
    return accumulated.reshape(slots, frames, height, widths, weights.shape[1])


def decode(
    entry_ext, feature_cache, live_lengths, entry_weight, block_weight, norm_gain, norm_shift
):
    latent_rim = padded(entry_ext, (("rows", 2),), 1)
    hidden = convolve(column_pad(latent_rim), entry_weight)
    slots, frames, height, widths, features = hidden.shape
    grouped = hidden.reshape(slots, frames, height, widths, GROUPS, features // GROUPS)
    group_sums = jnp.sum(grouped, axis=(2, 3, 5))
    squares = jnp.sum(grouped * grouped, axis=(2, 3, 5))
    group_sums, squares = lax.psum((group_sums, squares), "rows")
    cell_count = height * lax.axis_size("rows") * widths * (features // GROUPS)
    group_mean = group_sums / cell_count
    spread = squares / cell_count - group_mean * group_mean
    scaled = lax.rsqrt(spread + EPSILON)
    normed = (
        (grouped - group_mean[:, :, None, None, :, None]) * scaled[:, :, None, None, :, None]
    ).reshape(hidden.shape)
    normed = normed * norm_gain + norm_shift
    active = jax.nn.silu(normed).astype(jnp.bfloat16)
    stacked = jnp.concatenate([feature_cache, active], axis=1)
    bordered = column_pad(padded(stacked, (("rows", 2),), 1))
    mixed_sum = convolve(
        bordered, lax.all_gather(block_weight, ("roll", "rows"), axis=1, tiled=True)
    )
    alive_frames = jnp.arange(frames)[None, :] < live_lengths[:, None]
    return jnp.where(alive_frames[:, :, None, None, None], hidden + mixed_sum, 0.0).astype(
        jnp.bfloat16
    )


def on_device(
    latent_slabs,
    prior_latents,
    prior_features,
    lengths,
    starts,
    move_plan,
    entry_weight,
    block_weight,
    norm_gain,
    norm_shift,
):
    cached = starts > 0
    prior_lat = jnp.where(
        cached[:, None, None, None, None], prior_latents, jnp.zeros_like(prior_latents)
    )
    feature_cache = jnp.where(
        cached[:, None, None, None, None], prior_features, jnp.zeros_like(prior_features)
    )
    entry_ext = jnp.concatenate([prior_lat, latent_slabs], axis=1)
    live_lengths = jnp.where(move_plan >= 0, lengths, 0)
    return decode(
        entry_ext, feature_cache, live_lengths, entry_weight, block_weight, norm_gain, norm_shift
    )


def solution(mesh):
    in_specs = (
        P(("groups", "roll"), None, "rows", None, None),
        P(("groups", "roll"), None, "rows", None, None),
        P(("groups", "roll"), None, "rows", None, None),
        P(("groups", "roll")),
        P(("groups", "roll")),
        P(("groups", "roll")),
        P(),
        P(None, ("roll", "rows")),
        P(),
        P(),
    )
    out_specs = P(("groups", "roll"), None, "rows", None, None)
    return jax.shard_map(
        on_device, mesh=mesh, in_specs=in_specs, out_specs=out_specs, check_vma=False
    )
```

profile of v0, /device:TPU:0, one launch (start us, length us, event | category | flops | bytes accessed | tf_op | source)
XLA Modules:
  0.0 154.3 jit_solution(9679728959856541381)
XLA Ops:
  6.5 0.7 all-gather.2.cloned.1.call-update
  7.3 0.7 broadcast_compare_fusion
  7.9 0.9 broadcast_select_fusion.1
  8.8 0.7 pad_maximum_fusion.7
  9.6 5.0 %collective-permute-start = (bf16[2,5,1,8,16]{4,3,2,1,0:T(8,128)(2,1)S(1)}, bf16[2,5,1,8,16]{4,3,2,1,0:T(8,128)(2,1)S(1)}, u32[]{:S(2)}, u32[]{:S(2)}) collective-permute-start(bf16[2,5,1,8,16]{4,3,2,1,0:T(8,128)(2,1)S(1)} %get-tuple-element.67), channel_id=1, source_target_pairs={{0,1},{1,2},{2,3},{4,5},{5,6},{6,7},{8,9},{9,10},{10,11},{12,13},{... | collective-permute-start | bytes 7688 | tf_op jit(solution)/shard_map/ppermute | solution.py:19
  14.5 1.3 collective-permute-start.1
  15.8 0.7 compare_select_fusion
  16.6 1.0 broadcast_select_fusion
  17.6 0.9 pad_maximum_fusion.3
  18.5 1.7 %collective-permute-done.1 = bf16[2,5,1,8,16]{4,3,2,1,0:T(8,128)(2,1)S(1)} collective-permute-done((bf16[2,5,1,8,16]{4,3,2,1,0:T(8,128)(2,1)S(1)}, bf16[2,5,1,8,16]{4,3,2,1,0:T(8,128)(2,1)S(1)}, u32[]{:S(2)}, u32[]{:S(2)}) %collective-permute-start.1) | collective-permute-done | bytes 2592 | tf_op jit(solution)/shard_map/ppermute | solution.py:20
  20.2 1.1 pad_maximum_fusion.2
  21.3 1.1 select_maximum_fusion.2
  22.8 0.9 fusion.98
  23.8 0.9 convolution_add_fusion.33
  24.7 1.0 convolution_add_fusion.32
  25.7 1.0 convolution_add_fusion.31
  26.6 1.0 convolution_add_fusion.30
  32.8 4.1 %reshape_reshape.3 = f32[2,3,8,8,32,16]{5,4,3,2,1,0:T(8,128)} reshape(f32[384,512]{1,0:T(8,128)S(1)} %convolution_add_fusion.8) | data formatting | bytes 1572864 | tf_op jit(solution)/shard_map/reshape;reshape | solution.py:57
  36.9 4.1 %fusion.100 = (f32[2,3,32]{2,1,0:T(4,128)S(1)}, f32[2,3,32]{2,1,0:T(4,128)S(1)}) fusion(f32[2,3,8,8,32,16]{5,4,3,2,1,0:T(8,128)} %reshape_reshape.3), kind=kLoop, calls=%fused_computation.169 | loop fusion | flops 589440 | bytes 787968 | tf_op jit(solution)/shard_map/reduce_sum | solution.py:58
  41.0 12.3 %all-reduce.2 = (f32[2,3,32]{2,1,0:T(4,128)S(1)}, f32[2,3,32]{2,1,0:T(4,128)S(1)}) all-reduce(f32[2,3,32]{2,1,0:T(4,128)S(1)} %get-tuple-element.6, f32[2,3,32]{2,1,0:T(4,128)S(1)} %get-tuple-element.5), channel_id=1, replica_groups=mesh['groups'=2,'roll'=4,'rows'=4] {'rows'}, use_global_device_ids=true, to_apply=%region_3.4 | all-reduce | flops 384 | bytes 3072 | tf_op jit(solution)/shard_map/psum | solution.py:60
  53.8 1.0 multiply_convert_fusion
  55.1 1.3 collective-permute-start.2
  56.4 1.5 collective-permute-start.3
  57.9 0.9 fusion.70
  58.8 6.7 %collective-permute-done.3 = bf16[2,5,1,8,512]{4,3,2,1,0:T(8,128)(2,1)S(1)} collective-permute-done((bf16[2,5,1,8,512]{4,3,2,1,0:T(8,128)(2,1)S(1)}, bf16[2,5,1,8,512]{4,3,2,1,0:T(8,128)(2,1)S(1)}, u32[]{:S(2)}, u32[]{:S(2)}) %collective-permute-start.3) | collective-permute-done | bytes 81952 | tf_op jit(solution)/shard_map/ppermute | solution.py:20
  65.7 1.1 fusion.103
  66.7 1.0 fusion.102
  67.8 0.9 select_maximum_fusion
  68.7 2.4 %fusion.101 = (bf16[2,3,8,8,512]{4,3,2,1,0:T(8,128)(2,1)S(1)}, bf16[2,3,8,8,512]{4,3,2,1,0:T(8,128)(2,1)S(1)}, bf16[2,3,8,8,512]{4,3,2,1,0:T(8,128)(2,1)}, bf16[...) fusion(bf16[2,5,10,10,512]{4,3,2,1,0:T(8,128)(2,1)S(1)} %select, ...), kind=kLoop, calls=%fused_computation.170 | loop fusion | bytes 14155776 | tf_op jit(solution)/shard_map/slice | solution.py:40
  71.1 51.9 %all-gather.2.cloned.1.call-done = bf16[13824,512]{0,1:T(8,128)(2,1)} async-done(((bf16[13824,32]{0,1:T(8,128)(2,1)}), bf16[13824,512]{0,1:T(8,128)(2,1)}) %all-gather.2.cloned.1.call-update) | async-done | bytes 14155792 | tf_op jit(solution)/shard_map/all_gather | solution.py:73
  123.1 1.7 %fusion.54 = f32[384,512]{1,0:T(8,128)S(1)} fusion(bf16[384,512]{1,0:T(8,128)(2,1)} %bitcast.146, bf16[13824,512]{0,1:T(8,128)(2,1)} %all-gather.2.cloned.1.call-done), kind=kOutput, calls=%fused_computation.104 | convolution fusion | flops 201326592 | bytes 1703936 | tf_op jit(solution)/shard_map/dot_general | solution.py:43
  124.8 2.3 %fusion.59 = f32[384,512]{1,0:T(8,128)S(1)} fusion(bf16[384,512]{1,0:T(8,128)(2,1)} %bitcast.145, bf16[13824,512]{0,1:T(8,128)(2,1)} %all-gather.2.cloned.1.call-done), kind=kOutput, calls=%fused_computation.109 | convolution fusion | flops 201326592 | bytes 1703936 | tf_op jit(solution)/shard_map/dot_general | solution.py:43
  127.1 2.4 %fusion.61 = f32[384,512]{1,0:T(8,128)S(1)} fusion(bf16[384,512]{1,0:T(8,128)(2,1)} %bitcast.144, bf16[13824,512]{0,1:T(8,128)(2,1)} %all-gather.2.cloned.1.call-done), kind=kOutput, calls=%fused_computation.111 | convolution fusion | flops 201326592 | bytes 1703936 | tf_op jit(solution)/shard_map/dot_general | solution.py:43
  129.4 1.6 %fusion.65 = f32[384,512]{1,0:T(8,128)S(1)} fusion(bf16[384,512]{1,0:T(8,128)(2,1)} %bitcast.143, bf16[13824,512]{0,1:T(8,128)(2,1)} %all-gather.2.cloned.1.call-done), kind=kOutput, calls=%fused_computation.115 | convolution fusion | flops 201326592 | bytes 1703936 | tf_op jit(solution)/shard_map/dot_general | solution.py:43
  131.0 1.6 %fusion.52 = f32[384,512]{1,0:T(8,128)S(1)} fusion(bf16[384,512]{1,0:T(8,128)(2,1)} %bitcast.157, bf16[13824,512]{0,1:T(8,128)(2,1)} %all-gather.2.cloned.1.call-done), kind=kOutput, calls=%fused_computation.102 | convolution fusion | flops 201326592 | bytes 1703936 | tf_op jit(solution)/shard_map/dot_general | solution.py:43
  132.6 1.6 %fusion.63 = f32[384,512]{1,0:T(8,128)S(1)} fusion(bf16[384,512]{1,0:T(8,128)(2,1)} %bitcast.158, bf16[13824,512]{0,1:T(8,128)(2,1)} %all-gather.2.cloned.1.call-done), kind=kOutput, calls=%fused_computation.113 | convolution fusion | flops 201326592 | bytes 1703936 | tf_op jit(solution)/shard_map/dot_general | solution.py:43
  134.1 1.6 %fusion.57 = f32[384,512]{1,0:T(8,128)S(1)} fusion(bf16[384,512]{1,0:T(8,128)(2,1)} %bitcast.160, bf16[13824,512]{0,1:T(8,128)(2,1)} %all-gather.2.cloned.1.call-done), kind=kOutput, calls=%fused_computation.107 | convolution fusion | flops 201326592 | bytes 1703936 | tf_op jit(solution)/shard_map/dot_general | solution.py:43
  135.7 1.6 %fusion.49 = f32[384,512]{1,0:T(8,128)S(1)} fusion(bf16[384,512]{1,0:T(8,128)(2,1)} %bitcast.142, bf16[13824,512]{0,1:T(8,128)(2,1)} %all-gather.2.cloned.1.call-done), kind=kOutput, calls=%fused_computation.99 | convolution fusion | flops 201326592 | bytes 1703936 | tf_op jit(solution)/shard_map/dot_general | solution.py:43
  137.3 1.6 %fusion.47 = f32[384,512]{1,0:T(8,128)S(1)} fusion(bf16[384,512]{1,0:T(8,128)(2,1)} %bitcast.156, bf16[13824,512]{0,1:T(8,128)(2,1)} %all-gather.2.cloned.1.call-done), kind=kOutput, calls=%fused_computation.97 | convolution fusion | flops 201326592 | bytes 1703936 | tf_op jit(solution)/shard_map/dot_general | solution.py:43
  143.0 0.5 fusion.5
  143.5 0.4 fusion.7
  144.0 0.4 fusion.9
  144.4 0.4 fusion.11
  144.8 0.4 fusion.13
  145.3 0.4 fusion.15
  145.7 0.4 fusion.17
  146.1 0.4 convolution_add_fusion
  146.5 0.9 select_convert_fusion
  (82 shorter events, 10.3 us)
Async XLA Ops:
  6.5 21.1 %copy-start.13 = (bf16[432,512]{1,0:T(8,128)(2,1)S(1)}, bf16[432,512]{1,0:T(8,128)(2,1)}, u32[]{:S(2)}) copy-start(bf16[432,512]{1,0:T(8,128)(2,1)} %param.16) | copy-start | bytes 1327108
  6.5 116.5 %all-gather.2.cloned.1.call-start = ((), (), s32[]{:S(2)}) async-start(), calls=%async_computation | async-start | bytes 15040512 | tf_op jit(solution)/shard_map/all_gather | solution.py:73
  9.6 8.9 %collective-permute-start = (bf16[2,5,1,8,16]{4,3,2,1,0:T(8,128)(2,1)S(1)}, bf16[2,5,1,8,16]{4,3,2,1,0:T(8,128)(2,1)S(1)}, u32[]{:S(2)}, u32[]{:S(2)}) collective-permute-start(bf16[2,5,1,8,16]{4,3,2,1,0:T(8,128)(2,1)S(1)} %get-tuple-element.67), channel_id=1, source_target_pairs={{0,1},{1,2},{2,3},{4,5},{5,6},{6,7},{8,9},{9,10},{10,11},{12,13},{... | collective-permute-start | bytes 7688 | tf_op jit(solution)/shard_map/ppermute | solution.py:19
  14.5 5.7 %collective-permute-start.1 = (bf16[2,5,1,8,16]{4,3,2,1,0:T(8,128)(2,1)S(1)}, bf16[2,5,1,8,16]{4,3,2,1,0:T(8,128)(2,1)S(1)}, u32[]{:S(2)}, u32[]{:S(2)}) collective-permute-start(bf16[2,5,1,8,16]{4,3,2,1,0:T(8,128)(2,1)S(1)} %get-tuple-element.68), channel_id=1, source_target_pairs={{1,0},{2,1},{3,2},{5,4},{6,5},{7,6},{9,8},{10,9},{11,10},{13,12},{... | collective-permute-start | bytes 7688 | tf_op jit(solution)/shard_map/ppermute | solution.py:20
  27.6 4.0 %copy-start.1 = (bf16[2,3,8,8,16]{4,3,2,1,0:T(8,128)(2,1)S(1)}, bf16[2,3,8,8,16]{4,3,2,1,0:T(8,128)(2,1)}, u32[]{:S(2)}) copy-start(bf16[2,3,8,8,16]{4,3,2,1,0:T(8,128)(2,1)} %param.10) | copy-start | bytes 36868
  30.7 23.1 %copy-start.14 = (f32[512]{0:T(512)S(1)}, f32[512]{0:T(512)}, u32[]{:S(2)}) copy-start(f32[512]{0:T(512)} %param.19) | copy-start | bytes 6148
  30.7 23.1 %copy-start.15 = (f32[512]{0:T(512)S(1)}, f32[512]{0:T(512)}, u32[]{:S(2)}) copy-start(f32[512]{0:T(512)} %param.18) | copy-start | bytes 6148
  55.1 3.7 %collective-permute-start.2 = (bf16[2,5,1,8,512]{4,3,2,1,0:T(8,128)(2,1)S(1)}, bf16[2,5,1,8,512]{4,3,2,1,0:T(8,128)(2,1)S(1)}, u32[]{:S(2)}, u32[]{:S(2)}) collective-permute-start(bf16[2,5,1,8,512]{4,3,2,1,0:T(8,128)(2,1)S(1)} %get-tuple-element.37), channel_id=1, source_target_pairs={{0,1},{1,2},{2,3},{4,5},{5,6},{6,7},{8,9},{9,10},{10,11},{12,13},{... | collective-permute-start | bytes 245768 | tf_op jit(solution)/shard_map/ppermute | solution.py:19
  56.4 9.2 %collective-permute-start.3 = (bf16[2,5,1,8,512]{4,3,2,1,0:T(8,128)(2,1)S(1)}, bf16[2,5,1,8,512]{4,3,2,1,0:T(8,128)(2,1)S(1)}, u32[]{:S(2)}, u32[]{:S(2)}) collective-permute-start(bf16[2,5,1,8,512]{4,3,2,1,0:T(8,128)(2,1)S(1)} %get-tuple-element.38), channel_id=1, source_target_pairs={{1,0},{2,1},{3,2},{5,4},{6,5},{7,6},{9,8},{10,9},{11,10},{13,12},{... | collective-permute-start | bytes 245768 | tf_op jit(solution)/shard_map/ppermute | solution.py:20
  123.1 15.8 %copy-start = (bf16[13824,512]{0,1:T(8,128)(2,1)S(1)}, bf16[13824,512]{0,1:T(8,128)(2,1)}, u32[]{:S(2)}) copy-start(bf16[13824,512]{0,1:T(8,128)(2,1)} %all-gather.2.cloned.1.call-done) | copy-start | bytes 42467332
  123.1 16.2 %copy-start.12 = (bf16[2,3,8,8,512]{4,3,2,1,0:T(8,128)(2,1)S(1)}, bf16[2,3,8,8,512]{4,3,2,1,0:T(8,128)(2,1)}, u32[]{:S(2)}) copy-start(bf16[2,3,8,8,512]{4,3,2,1,0:T(8,128)(2,1)} %get-tuple-element.34) | copy-start | bytes 1179652
  123.1 17.1 %copy-start.9 = (bf16[2,3,8,8,512]{4,3,2,1,0:T(8,128)(2,1)S(1)}, bf16[2,3,8,8,512]{4,3,2,1,0:T(8,128)(2,1)}, u32[]{:S(2)}) copy-start(bf16[2,3,8,8,512]{4,3,2,1,0:T(8,128)(2,1)} %get-tuple-element.32) | copy-start | bytes 1179652
  123.1 17.9 %copy-start.10 = (bf16[2,3,8,8,512]{4,3,2,1,0:T(8,128)(2,1)S(1)}, bf16[2,3,8,8,512]{4,3,2,1,0:T(8,128)(2,1)}, u32[]{:S(2)}) copy-start(bf16[2,3,8,8,512]{4,3,2,1,0:T(8,128)(2,1)} %get-tuple-element.28) | copy-start | bytes 1179652
  123.1 18.3 %copy-start.11 = (bf16[384,512]{1,0:T(8,128)(2,1)S(1)}, bf16[384,512]{1,0:T(8,128)(2,1)}, u32[]{:S(2)}) copy-start(bf16[384,512]{1,0:T(8,128)(2,1)} %multiply_convert_fusion) | copy-start | bytes 1179652
  124.8 17.8 %copy-start.8 = (bf16[2,3,8,8,512]{4,3,2,1,0:T(8,128)(2,1)S(1)}, bf16[2,3,8,8,512]{4,3,2,1,0:T(8,128)(2,1)}, u32[]{:S(2)}) copy-start(bf16[2,3,8,8,512]{4,3,2,1,0:T(8,128)(2,1)} %get-tuple-element.31) | copy-start | bytes 1179652
  135.7 7.8 %copy-start.7 = (bf16[2,3,8,8,512]{4,3,2,1,0:T(8,128)(2,1)S(1)}, bf16[2,3,8,8,512]{4,3,2,1,0:T(8,128)(2,1)}, u32[]{:S(2)}) copy-start(bf16[2,3,8,8,512]{4,3,2,1,0:T(8,128)(2,1)} %get-tuple-element.21) | copy-start | bytes 1179652
  138.9 5.1 %copy-start.6 = (bf16[2,3,8,8,512]{4,3,2,1,0:T(8,128)(2,1)S(1)}, bf16[2,3,8,8,512]{4,3,2,1,0:T(8,128)(2,1)}, u32[]{:S(2)}) copy-start(bf16[2,3,8,8,512]{4,3,2,1,0:T(8,128)(2,1)} %get-tuple-element.19) | copy-start | bytes 1179652
  139.7 4.7 %copy-start.5 = (bf16[2,3,8,8,512]{4,3,2,1,0:T(8,128)(2,1)S(1)}, bf16[2,3,8,8,512]{4,3,2,1,0:T(8,128)(2,1)}, u32[]{:S(2)}) copy-start(bf16[2,3,8,8,512]{4,3,2,1,0:T(8,128)(2,1)} %get-tuple-element.17) | copy-start | bytes 1179652
  140.9 3.9 %copy-start.4 = (bf16[2,3,8,8,512]{4,3,2,1,0:T(8,128)(2,1)S(1)}, bf16[2,3,8,8,512]{4,3,2,1,0:T(8,128)(2,1)}, u32[]{:S(2)}) copy-start(bf16[2,3,8,8,512]{4,3,2,1,0:T(8,128)(2,1)} %get-tuple-element.15) | copy-start | bytes 1179652
  141.8 3.5 %copy-start.3 = (bf16[2,3,8,8,512]{4,3,2,1,0:T(8,128)(2,1)S(1)}, bf16[2,3,8,8,512]{4,3,2,1,0:T(8,128)(2,1)}, u32[]{:S(2)}) copy-start(bf16[2,3,8,8,512]{4,3,2,1,0:T(8,128)(2,1)} %get-tuple-element.13) | copy-start | bytes 1179652
  143.0 2.7 %copy-start.2 = (bf16[2,3,8,8,512]{4,3,2,1,0:T(8,128)(2,1)S(1)}, bf16[2,3,8,8,512]{4,3,2,1,0:T(8,128)(2,1)}, u32[]{:S(2)}) copy-start(bf16[2,3,8,8,512]{4,3,2,1,0:T(8,128)(2,1)} %get-tuple-element.11) | copy-start | bytes 1179652
Sparse Core Ops, SparseCore 0:
  9.6 113.3 all-gather.1
where the time goes:
time: 155 us; the launch traced here: 154 us
  waiting for transfers between devices  61.1 us (39%)
  matrix products  32.8 us (21%)
  other arithmetic  15.4 us (10%)
  between operations  14.2 us (9%)
  blocking collectives  12.3 us (8%)
  local copies, waits for them, and re-layouts  9.49 us (6%)
  starting transfers between devices  9.02 us (6%)
    all_gather x1, waiting for transfers between devices, decode(): lax.all_gather(block_weight, ('roll', 'rows'), axis=1, tiled=True)  51.9 us
    dot_general x54, matrix products, convolve(): jnp.dot(window.reshape(-1, channels), weights[tap_index * channels:(tap_i...  32.8 us
    psum x1, blocking collectives, decode(): group_sums, squares = lax.psum((group_sums, squares), 'rows')  12.3 us
    ppermute x2, waiting for transfers between devices, padded(): after = lax.ppermute(first, axis, down)  8.42 us
    ppermute x2, starting transfers between devices, padded(): before = lax.ppermute(last, axis, up)  6.25 us
    slice x5, local copies, waits for them, and re-layouts, convolve(): extended[:, step_t:step_t + frames, step_h:step_h + height, step_w:step_w...  4.93 us
    another operation x1, local copies, waits for them, and re-layouts, decode(): hidden.reshape(slots, frames, height, widths, GROUPS, features // GROUPS)  4.1 us
    reduce_sum x1, other arithmetic, decode(): group_sums = jnp.sum(grouped, axis=(2, 3, 5))  4.08 us
  transfers between devices with their start and end apart: 5, of which 3 were waited for; matrix products, arithmetic and copies ran while one was open for 22% of the time, Pallas kernels for 0%

commit v1 on v0

v1 whole, which is shorter than its diff:
```python
import functools

import jax
import jax.numpy as jnp
from jax import lax
from jax.experimental import pallas as pl
from jax.experimental.pallas import tpu as pltpu
from jax.sharding import PartitionSpec as P

GROUPS = 32
EPSILON = 1e-06
LANES = 128


def remote(src, dst, send, recv, axis, target):
    return pltpu.make_async_remote_copy(
        src_ref=src, dst_ref=dst, send_sem=send, recv_sem=recv,
        device_id={axis: target}, device_id_type=pl.DeviceIdType.MESH,
    )


def kernel(
    n_roll, n_rows, cw,
    live_ref, cached_ref, w_ref, pat_ref, feat_ref, we_ref, gain_ref, shift_ref,
    out_ref,
    wg, pg, fg, hid, xc, acc, res, got,
    own_sem, wsend, wrecv, fsend, frecv, psend, precv, gsend, grecv, rsend, rrecv,
):
    me = lax.axis_index("roll")
    row = lax.axis_index("rows")
    sibling = me + 1 - 2 * lax.rem(me, 2)
    half = n_roll // 2
    cwp = w_ref.shape[0]
    width = n_roll * cwp
    slabs, frames, cells, kdim = pat_ref.shape
    feats = gain_ref.shape[1]
    total = n_rows * cells
    chunk = w_ref.shape[1] // 3

    barrier = pltpu.get_barrier_semaphore()
    for s in range(1, n_rows):
        pl.semaphore_signal(barrier, inc=1, device_id={"rows": lax.rem(row + s, n_rows)},
                            device_id_type=pl.DeviceIdType.MESH)
    for s in range(1, half):
        pl.semaphore_signal(barrier, inc=1, device_id={"roll": lax.rem(me + 2 * s, n_roll)},
                            device_id_type=pl.DeviceIdType.MESH)
    pl.semaphore_signal(barrier, inc=1, device_id={"roll": sibling},
                        device_id_type=pl.DeviceIdType.MESH)
    pl.semaphore_wait(barrier, n_rows - 1 + half)

    def piece(ref, a):
        return ref.at[:, pl.ds(a * chunk, chunk)]

    def pat_copy(s):
        return remote(pat_ref, pg.at[row], psend.at[s], precv.at[s], "rows", lax.rem(row + s, n_rows))

    def pat_in(s):
        src = lax.rem(row - s + n_rows, n_rows)
        return remote(pat_ref, pg.at[src], psend.at[s], precv.at[s], "rows", lax.rem(row + s, n_rows))

    def feat_copy(s):
        return remote(feat_ref, fg.at[row], gsend.at[s], grecv.at[s], "rows", lax.rem(row + s, n_rows))

    def direct(s, a):
        return remote(piece(w_ref, a), piece(wg.at[me], a), wsend.at[s, a], wrecv.at[s, a],
                      "roll", lax.rem(me + 2 * s, n_roll))

    def forward(s, a):
        slot = lax.rem(me - 2 * s + n_roll, n_roll)
        src = w_ref if s == 0 else wg.at[slot]
        return remote(piece(src, a), piece(wg.at[slot], a), fsend.at[s, a], frecv.at[s, a],
                      "roll", sibling)

    own = [
        pltpu.make_async_copy(pat_ref, pg.at[row], own_sem.at[0]),
        pltpu.make_async_copy(feat_ref, fg.at[row], own_sem.at[1]),
        pltpu.make_async_copy(w_ref, wg.at[me], own_sem.at[2]),
    ]
    for c in own:
        c.start()
    for s in range(1, n_rows):
        pat_copy(s).start()
    for a in range(3):
        for s in range(1, half):
            direct(s, a).start()
        forward(0, a).start()
    for s in range(1, n_rows):
        feat_copy(s).start()

    own[0].wait()
    for s in range(1, n_rows):
        pat_copy(s).wait_recv()

    lane = lax.broadcasted_iota(jnp.int32, (8, feats), 1)
    sub = lax.broadcasted_iota(jnp.int32, (8, feats), 0)
    column = lax.rem(lax.broadcasted_iota(jnp.int32, (total, feats), 0), 8)
    group = feats // GROUPS
    count = float(total * group)

    def spread(s, f, start, v, col):
        size = v.shape[0]
        rows = pl.ds(start, size)
        xc[s, 1, f, rows, :] = v.astype(jnp.bfloat16)
        xc[s, 0, f, rows, :] = jnp.where(col == 0, 0.0, pltpu.roll(v, 1, 0)).astype(jnp.bfloat16)
        xc[s, 2, f, rows, :] = jnp.where(col == 7, 0.0, pltpu.roll(v, size - 1, 0)).astype(jnp.bfloat16)

    def entry(i, carry):
        s, t = i // frames, lax.rem(i, frames)
        p = jnp.concatenate([pg[z, s, t] for z in range(n_rows)], axis=0)
        ys = [jnp.dot(p, we_ref[b], preferred_element_type=jnp.float32) for b in range(3)]
        zero = jnp.zeros((8, feats), jnp.float32)
        h = (ys[1] + jnp.concatenate([zero, ys[0][:-8]], axis=0)
             + jnp.concatenate([ys[2][8:], zero], axis=0))
        hid[s, t] = h
        first = jnp.sum(h, axis=0, keepdims=True)
        second = jnp.sum(h * h, axis=0, keepdims=True)
        both = jnp.where(sub == 0, first, second)
        k = 1
        while k < group:
            other = jnp.where((lane // k) % 2 == 1, pltpu.roll(both, k, 1),
                              pltpu.roll(both, feats - k, 1))
            both = both + other
            k *= 2
        both = both / count
        mean, square = both[0:1], both[1:2]
        scaled = lax.rsqrt(square - mean * mean + EPSILON)
        v = (h - mean) * scaled * gain_ref[...] + shift_ref[...]
        v = v / (1.0 + jnp.exp(-v))
        spread(s, 2 + t, 0, v, column)
        return carry

    lax.fori_loop(0, slabs * frames // 2, entry, 0)
    for s in range(1, half):
        direct(s, 0).wait_recv()
        forward(s, 0).start()
    lax.fori_loop(slabs * frames // 2, slabs * frames, entry, 0)
    for s in range(1, half):
        direct(s, 1).wait_recv()
        forward(s, 1).start()

    own[1].wait()
    for s in range(1, n_rows):
        feat_copy(s).wait_recv()

    def cache(i, carry):
        s, f = i // 2, lax.rem(i, 2)
        for z in range(n_rows):
            v = fg[z, s, f].astype(jnp.float32)
            v = jnp.where(cached_ref[s] > 0, v, 0.0)
            spread(s, f, z * cells, v, column[:cells])
        return carry

    lax.fori_loop(0, slabs * 2, cache, 0)
    own[2].wait()

    for a in range(3):
        if a == 1:
            for s in range(1, half):
                direct(s, 2).wait_recv()
                forward(s, 2).start()
        for s in range(half):
            forward(s, a).wait_recv()

        def taps(s, carry):
            y = None
            for c in range(3):
                x = xc[s, c, a:a + frames].reshape(frames * total, feats)
                parts = []
                for b in range(3):
                    k0 = ((a * 3 + b) * 3 + c) * feats
                    parts.append(wg[:, :, k0:k0 + feats].reshape(width, feats))
                wmat = jnp.concatenate(parts, axis=0)
                d = lax.dot_general(x, wmat, (((1,), (1,)), ((), ())),
                                    preferred_element_type=jnp.float32)
                y = d if y is None else y + d
            acc[s] = y if a == 0 else acc[s] + y
            return carry

        lax.fori_loop(0, slabs, taps, 0)

    span = n_rows * cw
    tile_lane = lax.broadcasted_iota(jnp.int32, (total, LANES), 1)

    def finish(i, carry):
        s, t = i // frames, lax.rem(i, frames)
        rows = pl.ds(pl.multiple_of(t * total, total), total)
        y = [acc[s, rows, b * width:(b + 1) * width] for b in range(3)]
        zero = jnp.zeros((8, width), jnp.float32)
        m = (y[1] + jnp.concatenate([zero, y[0][:-8]], axis=0)
             + jnp.concatenate([y[2][8:], zero], axis=0))
        tiles = []
        for q in range(width // LANES):
            base = jnp.zeros((total, LANES), jnp.float32)
            for r in range(q * LANES // cwp, (q + 1) * LANES // cwp):
                tile = (r * span) // LANES
                offset = (r * span) % LANES + row * cw
                put = r * cwp - q * LANES
                h = hid[s, t, :, tile * LANES:(tile + 1) * LANES]
                h = pltpu.roll(h, lax.rem(put - offset + 2 * LANES, LANES), 1)
                base = jnp.where((tile_lane >= put) & (tile_lane < put + cw), h, base)
            tiles.append(base)
        hc = jnp.concatenate(tiles, axis=1) if len(tiles) > 1 else tiles[0]
        o = jnp.where(t < live_ref[s], m + hc, 0.0).astype(jnp.bfloat16)
        for z in range(n_rows):
            res[z, s, t] = o[z * cells:(z + 1) * cells]
        return carry

    lax.fori_loop(0, slabs * frames, finish, 0)

    def result(s):
        to = lax.rem(row + s, n_rows)
        return remote(res.at[to], got.at[row], rsend.at[s], rrecv.at[s], "rows", to)

    for s in range(1, n_rows):
        result(s).start()
    got[row] = res[row]
    for s in range(1, n_rows):
        result(s).wait_recv()
    out_ref[...] = got[...]

    for s in range(1, n_rows):
        pat_copy(s).wait_send()
        feat_copy(s).wait_send()
        result(s).wait_send()
    for a in range(3):
        for s in range(1, half):
            direct(s, a).wait_send()
        for s in range(half):
            forward(s, a).wait_send()


def on_device(
    latent_slabs, prior_latents, prior_features, lengths, starts, move_plan,
    entry_weight, block_weight, norm_gain, norm_shift,
):
    n_roll, n_rows = lax.axis_size("roll"), lax.axis_size("rows")
    slabs, frames, height, cols, lat = latent_slabs.shape
    feats = prior_features.shape[-1]
    cells = height * cols
    total = cells * n_rows
    cw = block_weight.shape[1]
    cwp = max(cw, 16)
    width = n_roll * cwp
    kdim = -(-9 * lat // LANES) * LANES
    cached = starts > 0
    prior = jnp.where(cached[:, None, None, None, None], prior_latents, jnp.zeros_like(prior_latents))
    ext = jnp.concatenate([prior, latent_slabs], axis=1)
    ext = jnp.pad(ext, ((0, 0), (0, 0), (0, 0), (1, 1), (0, 0)))
    taps = [ext[:, a:a + frames, :, c:c + cols, :] for a in range(3) for c in range(3)]
    pat = jnp.concatenate(taps, axis=-1)
    pat = jnp.pad(pat, ((0, 0),) * 4 + ((0, kdim - 9 * lat),)).reshape(slabs, frames, cells, kdim)
    we = entry_weight.reshape(3, 3, 3 * lat, feats).transpose(1, 0, 2, 3).reshape(3, 9 * lat, feats)
    we = jnp.pad(we, ((0, 0), (0, kdim - 9 * lat), (0, 0)))
    wt = block_weight.T
    if cwp != cw:
        wt = jnp.pad(wt, ((0, cwp - cw), (0, 0)))
    live = jnp.where(move_plan >= 0, lengths, 0)
    vm = pl.BlockSpec(memory_space=pltpu.VMEM)
    sm = pl.BlockSpec(memory_space=pltpu.SMEM)
    half = n_roll // 2
    dma = pltpu.SemaphoreType.DMA
    out = pl.pallas_call(
        functools.partial(kernel, n_roll, n_rows, cw),
        out_shape=jax.ShapeDtypeStruct((n_rows, slabs, frames, cells, width), jnp.bfloat16),
        in_specs=[sm, sm] + [vm] * 6,
        out_specs=vm,
        scratch_shapes=[
            pltpu.VMEM((n_roll, cwp, wt.shape[1]), jnp.bfloat16),
            pltpu.VMEM((n_rows, slabs, frames, cells, kdim), jnp.bfloat16),
            pltpu.VMEM((n_rows, slabs, 2, cells, feats), jnp.bfloat16),
            pltpu.VMEM((slabs, frames, total, feats), jnp.float32),
            pltpu.VMEM((slabs, 3, frames + 2, total, feats), jnp.bfloat16),
            pltpu.VMEM((slabs, frames * total, 3 * width), jnp.float32),
            pltpu.VMEM((n_rows, slabs, frames, cells, width), jnp.bfloat16),
            pltpu.VMEM((n_rows, slabs, frames, cells, width), jnp.bfloat16),
            dma((3,)),
            dma((half, 3)), dma((half, 3)), dma((half, 3)), dma((half, 3)),
            dma((n_rows,)), dma((n_rows,)), dma((n_rows,)), dma((n_rows,)),
            dma((n_rows,)), dma((n_rows,)),
        ],
        compiler_params=pltpu.CompilerParams(
            collective_id=0, has_side_effects=True, vmem_limit_bytes=67043328
        ),
        name="decode",
    )(
        live, cached.astype(jnp.int32), wt, pat,
        prior_features.reshape(slabs, 2, cells, feats), we,
        norm_gain[None], norm_shift[None],
    )
    out = out.reshape(n_rows, slabs, frames, cells, n_roll, cwp)[..., :cw]
    out = out.transpose(1, 2, 3, 4, 0, 5)
    return out.reshape(slabs, frames, height, cols, feats)


def solution(mesh):
    in_specs = (
        P(("groups", "roll"), None, "rows", None, None),
        P(("groups", "roll"), None, "rows", None, None),
        P(("groups", "roll"), None, "rows", None, None),
        P(("groups", "roll")),
        P(("groups", "roll")),
        P(("groups", "roll")),
        P(),
        P(None, ("roll", "rows")),
        P(),
        P(),
    )
    out_specs = P(("groups", "roll"), None, "rows", None, None)
    return jax.shard_map(
        on_device, mesh=mesh, in_specs=in_specs, out_specs=out_specs, check_vma=False
    )
```

time: 155 us -> 78.5 us (0.51)
  Pallas kernels: 0 us -> 65.4 us
  waiting for transfers between devices: 61.1 us -> 0 us
  matrix products: 32.8 us -> 0 us
  between operations: 14.2 us -> 0.05 us
  blocking collectives: 12.3 us -> 0 us
  other arithmetic: 15.4 us -> 4.45 us
  starting transfers between devices: 9.02 us -> 0 us
    pallas_call x0 -> x1, Pallas kernels: none -> 65.4 us  [on_device(): pl.pallas_call(functools.partial(kernel, n_roll, n_rows, cw), out_shape=j...]
    all_gather x1 -> x0, waiting for transfers between devices: 51.9 us -> none  [decode(): lax.all_gather(block_weight, ('roll', 'rows'), axis=1, tiled=True)]
    dot_general x54 -> x0, matrix products: 32.8 us -> none  [convolve(): jnp.dot(window.reshape(-1, channels), weights[tap_index * channels:(tap_i...]
    psum x1 -> x0, blocking collectives: 12.3 us -> none  [decode(): group_sums, squares = lax.psum((group_sums, squares), 'rows')]
    ppermute x4 -> x0, starting transfers between devices: 9.02 us -> none  [the longest x2 6.25 us: padded(): before = lax.ppermute(last, axis, up)]
    ppermute x4 -> x0, waiting for transfers between devices: 8.42 us -> none  [the longest x2 8.42 us: padded(): after = lax.ppermute(first, axis, down)]
    slice x5 -> x0, local copies, waits for them, and re-layouts: 4.93 us -> none  [convolve(): extended[:, step_t:step_t + frames, step_h:step_h + height, step_w:step_w...]
    another operation x1 -> x0, local copies, waits for them, and re-layouts: 4.1 us -> none  [decode(): hidden.reshape(slots, frames, height, widths, GROUPS, features // GROUPS)]
  transfers between devices with their start and end apart: 5 -> 0, of which waited for: 3 -> 0; matrix products, arithmetic and copies ran while one was open for 22% -> 0% of each run, Pallas kernels for 0% -> 0%
where the time goes in v1:
time: 78.5 us; the launch traced here: 78.1 us
  Pallas kernels  65.4 us (83%)
  local copies, waits for them, and re-layouts  8.2 us (10%)
  other arithmetic  4.45 us (6%)
    pallas_call x1, Pallas kernels, on_device(): pl.pallas_call(functools.partial(kernel, n_roll, n_rows, cw), out_shape=j...  65.4 us
    reshape x1, local copies, waits for them, and re-layouts, on_device(): return out.reshape(slabs, frames, height, cols, feats)  2.25 us

profile of v1, /device:TPU:0, one launch (start us, length us, event | category | flops | bytes accessed | tf_op | source)
XLA Modules:
  0.0 78.1 jit_solution(12120001019668640198)
XLA Ops:
  0.0 0.0 copy-start
  0.0 1.2 %compare_select_fusion.live_ref = s32[2]{0:T(128)} fusion(s32[2]{0:T(128)} %param.13, s32[2]{0:T(128)} %param.15), kind=kLoop, calls=%fused_computation.15 | loop fusion | flops 4 | bytes 24 | tf_op jit(solution)/shard_map/jit(_where)/select_n | solution.py:257
  1.2 1.2 %broadcast_compare_fusion = (pred[2]{0:T(512)(128)(4,1)S(1)}, s32[2]{0:T(128)}) fusion(s32[2]{0:T(128)} %param.14), kind=kLoop, calls=%fused_computation.16 | loop fusion | flops 4 | bytes 18 | tf_op jit(solution)/shard_map/gt | solution.py:245
  2.4 0.9 %broadcast_select_fusion = bf16[2,2,8,8,16]{4,3,2,1,0:T(8,128)(2,1)S(1)} fusion(bf16[2,2,8,8,16]{4,3,2,1,0:T(8,128)(2,1)} %param.11, pred[2]{0:T(512)(128)(4,1)S(1)} %get-tuple-element.13), kind=kLoop, calls=%fused_computation.14 | loop fusion | flops 4096 | bytes 16386 | tf_op jit(solution)/shard_map/jit(_where)/select_n | solution.py:246
  3.3 0.9 %pad_maximum_fusion = bf16[2,5,8,8,16]{4,3,2,1,0:T(8,128)(2,1)S(1)} fusion(bf16[2,2,8,8,16]{4,3,2,1,0:T(8,128)(2,1)S(1)} %broadcast_select_fusion, bf16[2,3,8,8,16]{4,3,2,1,0:T(8,128)(2,1)} %param.10), kind=kLoop, calls=%fused_computation.8 | loop fusion | flops 10240 | bytes 40960 | tf_op jit(solution)/shard_map/concatenate | solution.py:247
  4.3 1.0 %copy.13 = bf16[3,3,48,512]{3,2,0,1:T(8,128)(2,1)S(1)} copy(bf16[3,3,48,512]{3,2,1,0:T(8,128)(2,1)} %bitcast.16) | data formatting | bytes 884736 | tf_op jit(solution)/shard_map/reshape | solution.py:252
  5.3 1.0 %pad.14.we_ref = bf16[3,256,512]{2,1,0:T(8,128)(2,1)} pad(bf16[3,144,512]{2,1,0:T(8,128)(2,1)S(1)} %bitcast.14, bf16[]{:T(256)} %constant.1.clone.1), padding=0_0x0_112x0_0 | pad | bytes 1228802 | tf_op jit(solution)/shard_map/jit(_pad)/pad | solution.py:253
  6.3 0.0 copy-done
  6.3 0.2 pad_slice_fusion
  6.5 0.5 concatenate.7
  6.9 0.7 pad_bitcast_fusion.pat_ref
  7.6 65.4 %decode.1 = bf16[4,2,3,64,128]{4,3,2,1,0:T(8,128)(2,1)} custom-call(s32[2]{0:T(128)} %compare_select_fusion.live_ref, s32[2]{0:T(128)} %get-tuple-element.14.cached_ref, bf16[32,13824]{1,0:T(8,128)(2,1)} %bitcast.15, bf16[2,3,64,256]{3,2,1,0:T(8,128)(2,1)} %pad_bitcast_fusion.pat_ref, bf16[2,2,64,512]{3,2,1,0:T(8,128)(2,1)} %bitcast.17, ...), custom_call_target="tpu_custom_call" | custom-call | tf_op jit(solution)/shard_map/decode/pallas_call | solution.py:262
  73.1 1.4 %copy.14 = bf16[4,2,3,64,128]{3,4,2,1,0:T(8,128)(2,1)S(1)} copy(bf16[4,2,3,64,128]{4,3,2,1,0:T(8,128)(2,1)} %decode.1) | data formatting | bytes 786432 | tf_op jit(solution)/shard_map/decode/pallas_call | solution.py:262
  74.5 1.4 %copy.15 = bf16[2,3,64,4,4,32]{5,4,3,2,1,0:T(4,128)(2,1)S(1)} copy(bf16[2,3,64,4,4,32]{2,5,3,1,0,4:T(8,128)(2,1)S(1)} %bitcast.13) | data formatting | bytes 786432 | tf_op jit(solution)/shard_map/transpose | solution.py:291
  75.9 2.3 %reshape.24 = bf16[2,3,8,8,512]{4,3,2,1,0:T(8,128)(2,1)} reshape(bf16[2,3,64,4,4,32]{5,4,3,2,1,0:T(4,128)(2,1)S(1)} %copy.15) | data formatting | bytes 786432 | tf_op jit(solution)/shard_map/reshape | solution.py:292
Async XLA Ops:
  0.0 6.3 %copy-start = (bf16[2,3,8,8,16]{4,3,2,1,0:T(8,128)(2,1)S(1)}, bf16[2,3,8,8,16]{4,3,2,1,0:T(8,128)(2,1)}, u32[]{:S(2)}) copy-start(bf16[2,3,8,8,16]{4,3,2,1,0:T(8,128)(2,1)} %param.10) | copy-start | bytes 36868

commit v2 on v1

v2 whole, which is shorter than its diff:
```python
import functools

import jax
import jax.numpy as jnp
from jax import lax
from jax.experimental import pallas as pl
from jax.experimental.pallas import tpu as pltpu
from jax.sharding import PartitionSpec as P

GROUPS = 32
EPSILON = 1e-06
LANES = 128


def remote(src, dst, send, recv, axis, target):
    return pltpu.make_async_remote_copy(
        src_ref=src, dst_ref=dst, send_sem=send, recv_sem=recv,
        device_id={axis: target}, device_id_type=pl.DeviceIdType.MESH,
    )


def kernel(
    n_roll, n_rows, cw,
    lengths_ref, starts_ref, plan_ref, w_ref, lat_ref, feat_ref, ew_ref, gain_ref, shift_ref,
    out_ref,
    wg, lg, fg, wes, xs, hid, xc, acc, res, got,
    own_sem, wsend, wrecv, fsend, frecv, lsend, lrecv, gsend, grecv, rsend, rrecv,
):
    me = lax.axis_index("roll")
    row = lax.axis_index("rows")
    sibling = me + 1 - 2 * lax.rem(me, 2)
    half = n_roll // 2
    cwp = w_ref.shape[0]
    width = n_roll * cwp
    slabs, depth, height, dense = lat_ref.shape
    frames = depth - 2
    cols = feat_ref.shape[3]
    lat = dense // cols
    cells = height * cols
    feats = gain_ref.shape[1]
    total = n_rows * cells
    chunk = w_ref.shape[1] // 3

    barrier = pltpu.get_barrier_semaphore()
    for s in range(1, n_rows):
        pl.semaphore_signal(barrier, inc=1, device_id={"rows": lax.rem(row + s, n_rows)},
                            device_id_type=pl.DeviceIdType.MESH)
    for s in range(1, half):
        pl.semaphore_signal(barrier, inc=1, device_id={"roll": lax.rem(me + 2 * s, n_roll)},
                            device_id_type=pl.DeviceIdType.MESH)
    pl.semaphore_signal(barrier, inc=1, device_id={"roll": sibling},
                        device_id_type=pl.DeviceIdType.MESH)
    wes[...] = jnp.zeros_like(wes)
    for a in range(3):
        for b in range(3):
            k0 = (a * 3 + b) * 3 * lat
            wes[b, a * dense // 2:a * dense // 2 + 3 * lat] = ew_ref[k0:k0 + 3 * lat]
    pl.semaphore_wait(barrier, n_rows - 1 + half)

    def piece(ref, a):
        return ref.at[:, pl.ds(a * chunk, chunk)]

    def lat_copy(s):
        return remote(lat_ref, lg.at[row], lsend.at[s], lrecv.at[s], "rows", lax.rem(row + s, n_rows))

    def hop(k, way):
        src = lax.rem(row - way * k + n_rows, n_rows)
        to = lax.rem(row + way + n_rows, n_rows)
        d = 0 if way > 0 else 1
        return remote(feat_ref if k == 0 else fg.at[src], fg.at[src],
                      gsend.at[d, k], grecv.at[d, k], "rows", to)

    def sends(k, way):
        if way > 0:
            return (row >= k) & (row < n_rows - 1)
        return (row + k < n_rows) & (row > 0)

    def receives(k, way):
        return row > k if way > 0 else row + k + 1 < n_rows

    def relay(k):
        for way in (1, -1):
            if k > 0:
                @pl.when(receives(k - 1, way))
                def _():
                    hop(k - 1, way).wait_recv()
            if k < n_rows - 1:
                @pl.when(sends(k, way))
                def _():
                    hop(k, way).start()

    def direct(s, a):
        return remote(piece(w_ref, a), piece(wg.at[me], a), wsend.at[s, a], wrecv.at[s, a],
                      "roll", lax.rem(me + 2 * s, n_roll))

    def forward(s, a):
        slot = lax.rem(me - 2 * s + n_roll, n_roll)
        src = w_ref if s == 0 else wg.at[slot]
        return remote(piece(src, a), piece(wg.at[slot], a), fsend.at[s, a], frecv.at[s, a],
                      "roll", sibling)

    own = [
        pltpu.make_async_copy(lat_ref, lg.at[row], own_sem.at[0]),
        pltpu.make_async_copy(feat_ref, fg.at[row], own_sem.at[1]),
        pltpu.make_async_copy(w_ref, wg.at[me], own_sem.at[2]),
    ]
    for c in own:
        c.start()
    for s in range(1, n_rows):
        lat_copy(s).start()
    relay(0)
    order = (2, 1, 0)
    for a in order:
        for s in range(1, half):
            direct(s, a).start()
        forward(0, a).start()

    def pass_on(a):
        for s in range(1, half):
            direct(s, a).wait_recv()
            forward(s, a).start()

    own[0].wait()
    for s in range(1, n_rows):
        lat_copy(s).wait_recv()

    lane = lax.broadcasted_iota(jnp.int32, (8, feats), 1)
    sub = lax.broadcasted_iota(jnp.int32, (8, feats), 0)
    column = lax.rem(lax.broadcasted_iota(jnp.int32, (total, feats), 0), cols)
    group = feats // GROUPS
    count = float(total * group)
    high = n_rows * height
    at = lax.broadcasted_iota(jnp.int32, (high, cols, dense), 1)
    place = lax.broadcasted_iota(jnp.int32, (high, cols, dense), 2)
    keep = (place < 3 * lat) & ((at > 0) | (place >= lat)) & ((at < cols - 1) | (place < 2 * lat))

    def expand(i, carry):
        s, f = i // depth, lax.rem(i, depth)
        r = jnp.concatenate([lg[z, s, f].astype(jnp.float32) for z in range(n_rows)], axis=0)
        x = jnp.zeros((high, cols, dense), jnp.float32)
        for j in range(cols):
            move = (dense - lat * (j - 1)) % dense
            rj = pltpu.roll(r, move, 1) if move else r
            x = jnp.where(at == j, rj[:, None, :], x)
        x = jnp.where(keep & ((f >= 2) | (starts_ref[s] > 0)), x, 0.0)
        xs[s, f] = x.reshape(total, dense)
        return carry

    lax.fori_loop(0, slabs * depth, expand, 0)

    def spread(s, f, start, v, col):
        size = v.shape[0]
        rows = pl.ds(start, size)
        xc[s, 1, f, rows, :] = v.astype(jnp.bfloat16)
        xc[s, 0, f, rows, :] = jnp.where(col == 0, 0.0, pltpu.roll(v, 1, 0)).astype(jnp.bfloat16)
        xc[s, 2, f, rows, :] = jnp.where(
            col == cols - 1, 0.0, pltpu.roll(v, size - 1, 0)).astype(jnp.bfloat16)

    def entry(i, carry):
        s, t = i // frames, lax.rem(i, frames)
        p = jnp.concatenate(
            [xs[s, t] + pltpu.roll(xs[s, t + 1], dense // 2, 1), xs[s, t + 2]], axis=1
        ).astype(jnp.bfloat16)
        ys = [jnp.dot(p, wes[b], preferred_element_type=jnp.float32) for b in range(3)]
        zero = jnp.zeros((cols, feats), jnp.float32)
        h = (ys[1] + jnp.concatenate([zero, ys[0][:-cols]], axis=0)
             + jnp.concatenate([ys[2][cols:], zero], axis=0))
        hid[s, t] = h
        first = jnp.sum(h, axis=0, keepdims=True)
        second = jnp.sum(h * h, axis=0, keepdims=True)
        both = jnp.where(sub == 0, first, second)
        k = 1
        while k < group:
            other = jnp.where((lane // k) % 2 == 1, pltpu.roll(both, k, 1),
                              pltpu.roll(both, feats - k, 1))
            both = both + other
            k *= 2
        both = both / count
        mean, square = both[0:1], both[1:2]
        scaled = lax.rsqrt(square - mean * mean + EPSILON)
        v = (h - mean) * scaled * gain_ref[...] + shift_ref[...]
        v = v / (1.0 + jnp.exp(-v))
        spread(s, 2 + t, 0, v, column)
        return carry

    lax.fori_loop(0, slabs * frames // 2, entry, 0)
    relay(1)
    pass_on(order[0])
    lax.fori_loop(slabs * frames // 2, slabs * frames, entry, 0)
    relay(2)
    pass_on(order[1])
    own[2].wait()

    def arrive(a):
        for s in range(half):
            forward(s, a).wait_recv()

    def taps(a, s):
        y = None
        for c in range(3):
            x = xc[s, c, a:a + frames].reshape(frames * total, feats)
            parts = []
            for b in range(3):
                k0 = ((a * 3 + b) * 3 + c) * feats
                parts.append(wg[:, :, k0:k0 + feats].reshape(width, feats))
            wmat = jnp.concatenate(parts, axis=0)
            d = lax.dot_general(x, wmat, (((1,), (1,)), ((), ())),
                                preferred_element_type=jnp.float32)
            y = d if y is None else y + d
        acc[s] = y if a == order[0] else acc[s] + y

    def each(a):
        def body(s, carry):
            taps(a, s)
            return carry
        lax.fori_loop(0, slabs, body, 0)

    arrive(order[0])
    each(order[0])

    for k in range(3, n_rows):
        relay(k)
    own[1].wait()

    def cache(i, carry):
        s, f = i // 2, lax.rem(i, 2)
        for z in range(n_rows):
            v = fg[z, s, f].astype(jnp.float32).reshape(cells, feats)
            v = jnp.where(starts_ref[s] > 0, v, 0.0)
            spread(s, f, z * cells, v, column[:cells])
        return carry

    lax.fori_loop(0, slabs * 2, cache, 0)
    pass_on(order[2])
    arrive(order[1])
    each(order[1])
    arrive(order[2])

    span = n_rows * cw
    tile_lane = lax.broadcasted_iota(jnp.int32, (total, LANES), 1)

    def finish(s, t):
        rows = pl.ds(pl.multiple_of(t * total, total), total)
        y = [acc[s, rows, b * width:(b + 1) * width] for b in range(3)]
        zero = jnp.zeros((cols, width), jnp.float32)
        m = (y[1] + jnp.concatenate([zero, y[0][:-cols]], axis=0)
             + jnp.concatenate([y[2][cols:], zero], axis=0))
        tiles = []
        for q in range(width // LANES):
            base = jnp.zeros((total, LANES), jnp.float32)
            for r in range(q * LANES // cwp, (q + 1) * LANES // cwp):
                tile = (r * span) // LANES
                offset = (r * span) % LANES + row * cw
                put = r * cwp - q * LANES
                h = hid[s, t, :, tile * LANES:(tile + 1) * LANES]
                h = pltpu.roll(h, lax.rem(put - offset + 2 * LANES, LANES), 1)
                base = jnp.where((tile_lane >= put) & (tile_lane < put + cw), h, base)
            tiles.append(base)
        hc = jnp.concatenate(tiles, axis=1) if len(tiles) > 1 else tiles[0]
        live = (plan_ref[s] >= 0) & (t < lengths_ref[s])
        o = jnp.where(live, m + hc, 0.0).astype(jnp.bfloat16)
        for z in range(n_rows):
            res[s, z, t] = o[z * cells:(z + 1) * cells]

    def result(s, k):
        to = lax.rem(row + k, n_rows)
        return remote(res.at[s, to], got.at[s, row], rsend.at[s, k], rrecv.at[s, k], "rows", to)

    for s in range(slabs):
        taps(order[2], s)

        def close(t, carry, s=s):
            finish(s, t)
            return carry

        lax.fori_loop(0, frames, close, 0)
        for k in range(1, n_rows):
            result(s, k).start()
        got[s, row] = res[s, row]

    owner_lane = lax.broadcasted_iota(jnp.int32, (cells, LANES), 1)
    for s in range(slabs):
        for k in range(1, n_rows):
            result(s, k).wait_recv()

        def gather(t, carry, s=s):
            tiles = [jnp.zeros((cells, LANES), jnp.float32) for _ in range(feats // LANES)]
            for z in range(n_rows):
                g = got[s, z, t].astype(jnp.float32)
                for r in range(n_roll):
                    q, take = (r * cwp) // LANES, (r * cwp) % LANES
                    start = (r * n_rows + z) * cw
                    tile, put = start // LANES, start % LANES
                    h = g[:, q * LANES:(q + 1) * LANES]
                    move = (put - take) % LANES
                    if move:
                        h = pltpu.roll(h, move, 1)
                    tiles[tile] = jnp.where(
                        (owner_lane >= put) & (owner_lane < put + cw), h, tiles[tile])
            o = jnp.concatenate(tiles, axis=1)
            out_ref[s, t] = o.reshape(height, cols, feats).astype(jnp.bfloat16)
            return carry

        lax.fori_loop(0, frames, gather, 0)

    for s in range(1, n_rows):
        lat_copy(s).wait_send()
        for i in range(slabs):
            result(i, s).wait_send()
    for k in range(n_rows - 1):
        for way in (1, -1):
            @pl.when(sends(k, way))
            def _():
                hop(k, way).wait_send()
    for a in range(3):
        for s in range(1, half):
            direct(s, a).wait_send()
        for s in range(half):
            forward(s, a).wait_send()


def on_device(
    latent_slabs, prior_latents, prior_features, lengths, starts, move_plan,
    entry_weight, block_weight, norm_gain, norm_shift,
):
    n_roll, n_rows = lax.axis_size("roll"), lax.axis_size("rows")
    slabs, frames, height, cols, lat = latent_slabs.shape
    feats = prior_features.shape[-1]
    cells = height * cols
    total = cells * n_rows
    dense = cols * lat
    cw = block_weight.shape[1]
    cwp = max(cw, 16)
    width = n_roll * cwp
    dense_lat = jnp.concatenate([prior_latents, latent_slabs], axis=1).reshape(
        slabs, frames + 2, height, dense)
    wt = block_weight.T
    if cwp != cw:
        wt = jnp.pad(wt, ((0, cwp - cw), (0, 0)))
    vm = pl.BlockSpec(memory_space=pltpu.VMEM)
    sm = pl.BlockSpec(memory_space=pltpu.SMEM)
    half = n_roll // 2
    dma = pltpu.SemaphoreType.DMA
    return pl.pallas_call(
        functools.partial(kernel, n_roll, n_rows, cw),
        out_shape=jax.ShapeDtypeStruct((slabs, frames, height, cols, feats), jnp.bfloat16),
        in_specs=[sm] * 3 + [vm] * 6,
        out_specs=vm,
        scratch_shapes=[
            pltpu.VMEM((n_roll, cwp, wt.shape[1]), jnp.bfloat16),
            pltpu.VMEM((n_rows, slabs, frames + 2, height, dense), jnp.bfloat16),
            pltpu.VMEM((n_rows, slabs, 2, height, cols, feats), jnp.bfloat16),
            pltpu.VMEM((3, 2 * dense, feats), jnp.bfloat16),
            pltpu.VMEM((slabs, frames + 2, total, dense), jnp.float32),
            pltpu.VMEM((slabs, frames, total, feats), jnp.float32),
            pltpu.VMEM((slabs, 3, frames + 2, total, feats), jnp.bfloat16),
            pltpu.VMEM((slabs, frames * total, 3 * width), jnp.float32),
            pltpu.VMEM((slabs, n_rows, frames, cells, width), jnp.bfloat16),
            pltpu.VMEM((slabs, n_rows, frames, cells, width), jnp.bfloat16),
            dma((3,)),
            dma((half, 3)), dma((half, 3)), dma((half, 3)), dma((half, 3)),
            dma((n_rows,)), dma((n_rows,)),
            dma((2, n_rows)), dma((2, n_rows)),
            dma((slabs, n_rows)), dma((slabs, n_rows)),
        ],
        compiler_params=pltpu.CompilerParams(
            collective_id=0, has_side_effects=True, vmem_limit_bytes=67043328
        ),
        name="decode",
    )(
        lengths, starts, move_plan, wt, dense_lat, prior_features, entry_weight,
        norm_gain[None], norm_shift[None],
    )


def solution(mesh):
    in_specs = (
        P(("groups", "roll"), None, "rows", None, None),
        P(("groups", "roll"), None, "rows", None, None),
        P(("groups", "roll"), None, "rows", None, None),
        P(("groups", "roll")),
        P(("groups", "roll")),
        P(("groups", "roll")),
        P(),
        P(None, ("roll", "rows")),
        P(),
        P(),
    )
    out_specs = P(("groups", "roll"), None, "rows", None, None)
    return jax.shard_map(
        on_device, mesh=mesh, in_specs=in_specs, out_specs=out_specs, check_vma=False
    )
```

time: 78.5 us -> 46.9 us (0.60)
  Pallas kernels: 65.4 us -> 43.2 us
  local copies, waits for them, and re-layouts: 8.2 us -> 2.53 us
  other arithmetic: 4.45 us -> 0.93 us
    pallas_call x1, Pallas kernels: 65.4 us -> 43.2 us  [on_device(): pl.pallas_call(functools.partial(kernel, n_roll, n_rows, cw), out_shape=j...]
    reshape x3 -> x1, local copies, waits for them, and re-layouts: 4 us -> 0.76 us  [on_device(): jnp.concatenate([prior_latents, latent_slabs], axis=1)]
    select_n x2 -> x0, other arithmetic: 2.16 us -> none  [the longest x1 1.24 us: on_device(): live = jnp.where(move_plan >= 0, lengths, 0)]
    unnamed x2 -> x1, local copies, waits for them, and re-layouts: 0.01 us -> 1.78 us
    transpose x1 -> x0, local copies, waits for them, and re-layouts: 1.4 us -> none  [on_device(): out = out.transpose(1, 2, 3, 4, 0, 5)]
    pallas_call x1 -> x0, local copies, waits for them, and re-layouts: 1.37 us -> none  [on_device(): pl.pallas_call(functools.partial(kernel, n_roll, n_rows, cw), out_shape=j...]
    gt x1 -> x0, other arithmetic: 1.16 us -> none  [on_device(): cached = starts > 0]
    pad x1 -> x0, local copies, waits for them, and re-layouts: 0.96 us -> none  [on_device(): we = jnp.pad(we, ((0, 0), (0, kdim - 9 * lat), (0, 0)))]
where the time goes in v2:
time: 46.9 us; the launch traced here: 46.7 us
  Pallas kernels  43.2 us (92%)
  local copies, waits for them, and re-layouts  2.53 us (5%)
  other arithmetic  0.93 us (2%)
    pallas_call x1, Pallas kernels, on_device(): pl.pallas_call(functools.partial(kernel, n_roll, n_rows, cw), out_shape=j...  43.2 us
    unnamed x1, local copies, waits for them, and re-layouts  1.78 us

profile of v2, /device:TPU:0, one launch (start us, length us, event | category | flops | bytes accessed | tf_op | source)
XLA Modules:
  0.0 46.7 jit_solution(2358223469277783188)
XLA Ops:
  0.0 0.9 %pad_maximum_fusion = bf16[2,5,8,8,16]{4,3,2,1,0:T(8,128)(2,1)S(1)} fusion(bf16[2,3,8,8,16]{4,3,2,1,0:T(8,128)(2,1)} %param.10, bf16[2,2,8,8,16]{4,3,2,1,0:T(8,128)(2,1)} %param.11), kind=kLoop, calls=%fused_computation | loop fusion | flops 10240 | bytes 40960 | tf_op jit(solution)/shard_map/concatenate | solution.py:335
  0.9 0.8 %reshape.3.lat_ref = bf16[2,5,8,128]{3,2,1,0:T(8,128)(2,1)} reshape(bf16[2,5,8,8,16]{4,3,2,1,0:T(8,128)(2,1)S(1)} %pad_maximum_fusion) | data formatting | bytes 40960 | tf_op jit(solution)/shard_map/reshape | solution.py:335
  1.7 43.2 %decode.1 = bf16[2,3,8,8,512]{4,3,2,1,0:T(8,128)(2,1)} custom-call(s32[2]{0:T(128)} %lengths_ref.1, s32[2]{0:T(128)} %starts_ref.1, s32[2]{0:T(128)} %plan_ref.1, bf16[32,13824]{1,0:T(8,128)(2,1)} %bitcast.5, bf16[2,5,8,128]{3,2,1,0:T(8,128)(2,1)} %reshape.3.lat_ref, bf16[2,2,8,8,512]{4,3,2,1,0:T(8,128)(2,1)} %feat_ref.1, bf16[432,512]{1,0:T(8,128)(2,1)} %ew_ref.1, ...), custom_call_target="tpu_custom_call" | custom-call | tf_op jit(solution)/shard_map/decode/pallas_call | solution.py:344
  44.9 1.8 %copy.12 = bf16[2,3,8,8,512]{4,3,2,1,0:T(8,128)(2,1)} copy(bf16[2,3,8,8,512]{4,3,2,1,0:T(8,128)(2,1)} %decode.1) | data formatting | bytes 786432

commit v3 on v2

--- a/solution.py
+++ b/solution.py
@@ -20,14 +20,15 @@
 
 
 def kernel(
-    n_roll, n_rows, cw,
+    n_groups, n_roll, n_rows, cw,
     lengths_ref, starts_ref, plan_ref, w_ref, lat_ref, feat_ref, ew_ref, gain_ref, shift_ref,
     out_ref,
     wg, lg, fg, wes, xs, hid, xc, acc, res, got,
-    own_sem, wsend, wrecv, fsend, frecv, lsend, lrecv, gsend, grecv, rsend, rrecv,
+    own_sem, wsend, wrecv, xsend, xrecv, fsend, frecv, lsend, lrecv, gsend, grecv, rsend, rrecv,
 ):
     me = lax.axis_index("roll")
     row = lax.axis_index("rows")
+    mine = lax.axis_index("groups") if n_groups == 2 else 0
     sibling = me + 1 - 2 * lax.rem(me, 2)
     half = n_roll // 2
     cwp = w_ref.shape[0]
@@ -40,6 +41,7 @@
     feats = gain_ref.shape[1]
     total = n_rows * cells
     chunk = w_ref.shape[1] // 3
+    part = chunk // n_groups if n_groups == 2 else chunk
 
     barrier = pltpu.get_barrier_semaphore()
     for s in range(1, n_rows):
@@ -50,12 +52,15 @@
                             device_id_type=pl.DeviceIdType.MESH)
     pl.semaphore_signal(barrier, inc=1, device_id={"roll": sibling},
                         device_id_type=pl.DeviceIdType.MESH)
+    if n_groups == 2:
+        pl.semaphore_signal(barrier, inc=1, device_id={"groups": 1 - mine},
+                            device_id_type=pl.DeviceIdType.MESH)
     wes[...] = jnp.zeros_like(wes)
     for a in range(3):
         for b in range(3):
             k0 = (a * 3 + b) * 3 * lat
             wes[b, a * dense // 2:a * dense // 2 + 3 * lat] = ew_ref[k0:k0 + 3 * lat]
-    pl.semaphore_wait(barrier, n_rows - 1 + half)
+    pl.semaphore_wait(barrier, n_rows - 1 + half + (n_groups == 2))
 
     def piece(ref, a):
         return ref.at[:, pl.ds(a * chunk, chunk)]
@@ -89,15 +94,27 @@
                 def _():
                     hop(k, way).start()
 
+    def share(ref, a, h):
+        return ref.at[:, pl.ds(pl.multiple_of(a * chunk + h * part, LANES), part)]
+
     def direct(s, a):
-        return remote(piece(w_ref, a), piece(wg.at[me], a), wsend.at[s, a], wrecv.at[s, a],
-                      "roll", lax.rem(me + 2 * s, n_roll))
-
-    def forward(s, a):
-        slot = lax.rem(me - 2 * s + n_roll, n_roll)
-        src = w_ref if s == 0 else wg.at[slot]
-        return remote(piece(src, a), piece(wg.at[slot], a), fsend.at[s, a], frecv.at[s, a],
+        return remote(share(w_ref, a, mine), share(wg.at[me], a, mine), wsend.at[s, a],
+                      wrecv.at[s, a], "roll", lax.rem(me + 2 * s, n_roll))
+
+    def slot_of(s):
+        return lax.rem(me - 2 * s + n_roll, n_roll)
+
+    def swap(s, a):
+        block = share(wg.at[slot_of(s)], a, mine)
+        return remote(block, block, xsend.at[s, a], xrecv.at[s, a], "groups", 1 - mine)
+
+    def give(a):
+        return remote(piece(w_ref, a), piece(wg.at[me], a), fsend.at[0, 0, a], frecv.at[0, 0, a],
                       "roll", sibling)
+
+    def forward(s, a, u):
+        block = share(wg.at[slot_of(s)], a, mine if u == 0 else 1 - mine)
+        return remote(block, block, fsend.at[u, s, a], frecv.at[u, s, a], "roll", sibling)
 
     own = [
         pltpu.make_async_copy(lat_ref, lg.at[row], own_sem.at[0]),
@@ -109,16 +126,23 @@
     for s in range(1, n_rows):
         lat_copy(s).start()
     relay(0)
-    order = (2, 1, 0)
-    for a in order:
+    for a in (2, 1, 0):
         for s in range(1, half):
             direct(s, a).start()
-        forward(0, a).start()
+        give(a).start()
 
     def pass_on(a):
         for s in range(1, half):
             direct(s, a).wait_recv()
-            forward(s, a).start()
+            if n_groups == 2:
+                swap(s, a).start()
+            forward(s, a, 0).start()
+
+    def pass_swap(a):
+        if n_groups == 2:
+            for s in range(1, half):
+                swap(s, a).wait_recv()
+                forward(s, a, 1).start()
 
     own[0].wait()
     for s in range(1, n_rows):
@@ -183,22 +207,29 @@
         spread(s, 2 + t, 0, v, column)
         return carry
 
-    lax.fori_loop(0, slabs * frames // 2, entry, 0)
+    jobs = slabs * frames
+    lax.fori_loop(0, jobs // 3, entry, 0)
+    pass_on(2)
+    lax.fori_loop(jobs // 3, 2 * jobs // 3, entry, 0)
+    pass_on(1)
     relay(1)
-    pass_on(order[0])
-    lax.fori_loop(slabs * frames // 2, slabs * frames, entry, 0)
-    relay(2)
-    pass_on(order[1])
+    pass_swap(2)
+    lax.fori_loop(2 * jobs // 3, jobs, entry, 0)
+    pass_on(0)
+    pass_swap(1)
     own[2].wait()
 
     def arrive(a):
-        for s in range(half):
-            forward(s, a).wait_recv()
-
-    def taps(a, s):
+        give(a).wait_recv()
+        for s in range(1, half):
+            forward(s, a, 0).wait_recv()
+            if n_groups == 2:
+                forward(s, a, 1).wait_recv()
+
+    def taps(a, s, t0, t1):
         y = None
         for c in range(3):
-            x = xc[s, c, a:a + frames].reshape(frames * total, feats)
+            x = xc[s, c, a + t0:a + t1].reshape((t1 - t0) * total, feats)
             parts = []
             for b in range(3):
                 k0 = ((a * 3 + b) * 3 + c) * feats
@@ -207,40 +238,28 @@
             d = lax.dot_general(x, wmat, (((1,), (1,)), ((), ())),
                                 preferred_element_type=jnp.float32)
             y = d if y is None else y + d
-        acc[s] = y if a == order[0] else acc[s] + y
-
-    def each(a):
+        rows = slice(t0 * total, t1 * total)
+        acc[s, rows] = y if a == 2 else acc[s, rows] + y
+
+    def each(a, t0, t1):
         def body(s, carry):
-            taps(a, s)
+            taps(a, s, t0, t1)
             return carry
         lax.fori_loop(0, slabs, body, 0)
 
-    arrive(order[0])
-    each(order[0])
-
-    for k in range(3, n_rows):
-        relay(k)
-    own[1].wait()
-
-    def cache(i, carry):
-        s, f = i // 2, lax.rem(i, 2)
-        for z in range(n_rows):
-            v = fg[z, s, f].astype(jnp.float32).reshape(cells, feats)
-            v = jnp.where(starts_ref[s] > 0, v, 0.0)
-            spread(s, f, z * cells, v, column[:cells])
-        return carry
-
-    lax.fori_loop(0, slabs * 2, cache, 0)
-    pass_on(order[2])
-    arrive(order[1])
-    each(order[1])
-    arrive(order[2])
+    arrive(2)
+    each(2, 0, frames)
+    relay(2)
+    pass_swap(0)
+    arrive(1)
+    each(1, 1, frames)
+    arrive(0)
 
     span = n_rows * cw
     tile_lane = lax.broadcasted_iota(jnp.int32, (total, LANES), 1)
 
     def finish(s, t):
-        rows = pl.ds(pl.multiple_of(t * total, total), total)
+        rows = pl.ds(t * total, total)
         y = [acc[s, rows, b * width:(b + 1) * width] for b in range(3)]
         zero = jnp.zeros((cols, width), jnp.float32)
         m = (y[1] + jnp.concatenate([zero, y[0][:-cols]], axis=0)
@@ -262,61 +281,91 @@
         for z in range(n_rows):
             res[s, z, t] = o[z * cells:(z + 1) * cells]
 
-    def result(s, k):
+    def late(u):
+        return pl.ds(2, frames - 2) if u == 0 else pl.ds(0, 2)
+
+    def result(s, u, k):
         to = lax.rem(row + k, n_rows)
-        return remote(res.at[s, to], got.at[s, row], rsend.at[s, k], rrecv.at[s, k], "rows", to)
+        return remote(res.at[s, to, late(u)], got.at[s, row, late(u)],
+                      rsend.at[s, u, k], rrecv.at[s, u, k], "rows", to)
+
+    def close(s, u):
+        for t in range(2, frames) if u == 0 else range(2):
+            finish(s, t)
+        for k in range(1, n_rows):
+            result(s, u, k).start()
+        got[s, row, late(u)] = res[s, row, late(u)]
 
     for s in range(slabs):
-        taps(order[2], s)
-
-        def close(t, carry, s=s):
-            finish(s, t)
-            return carry
-
-        lax.fori_loop(0, frames, close, 0)
-        for k in range(1, n_rows):
-            result(s, k).start()
-        got[s, row] = res[s, row]
+        taps(0, s, 2, frames)
+        close(s, 0)
+
+    for k in range(3, n_rows):
+        relay(k)
+    own[1].wait()
+
+    def cache(i, carry):
+        s, f = i // 2, lax.rem(i, 2)
+        for z in range(n_rows):
+            v = fg[z, s, f].astype(jnp.float32).reshape(cells, feats)
+            v = jnp.where(starts_ref[s] > 0, v, 0.0)
+            spread(s, f, z * cells, v, column[:cells])
+        return carry
+
+    lax.fori_loop(0, slabs * 2, cache, 0)
+    for s in range(slabs):
+        taps(1, s, 0, 1)
+        taps(0, s, 0, 2)
+        close(s, 1)
 
     owner_lane = lax.broadcasted_iota(jnp.int32, (cells, LANES), 1)
-    for s in range(slabs):
-        for k in range(1, n_rows):
-            result(s, k).wait_recv()
-
-        def gather(t, carry, s=s):
-            tiles = [jnp.zeros((cells, LANES), jnp.float32) for _ in range(feats // LANES)]
-            for z in range(n_rows):
-                g = got[s, z, t].astype(jnp.float32)
-                for r in range(n_roll):
-                    q, take = (r * cwp) // LANES, (r * cwp) % LANES
-                    start = (r * n_rows + z) * cw
-                    tile, put = start // LANES, start % LANES
-                    h = g[:, q * LANES:(q + 1) * LANES]
-                    move = (put - take) % LANES
-                    if move:
-                        h = pltpu.roll(h, move, 1)
-                    tiles[tile] = jnp.where(
-                        (owner_lane >= put) & (owner_lane < put + cw), h, tiles[tile])
-            o = jnp.concatenate(tiles, axis=1)
-            out_ref[s, t] = o.reshape(height, cols, feats).astype(jnp.bfloat16)
-            return carry
-
-        lax.fori_loop(0, frames, gather, 0)
+
+    def placed(s, t):
+        tiles = [jnp.zeros((cells, LANES), jnp.float32) for _ in range(feats // LANES)]
+        for z in range(n_rows):
+            g = got[s, z, t].astype(jnp.float32)
+            for r in range(n_roll):
+                q, take = (r * cwp) // LANES, (r * cwp) % LANES
+                start = (r * n_rows + z) * cw
+                tile, put = start // LANES, start % LANES
+                h = g[:, q * LANES:(q + 1) * LANES]
+                move = (put - take) % LANES
+                if move:
+                    h = pltpu.roll(h, move, 1)
+                tiles[tile] = jnp.where(
+                    (owner_lane >= put) & (owner_lane < put + cw), h, tiles[tile])
+        o = jnp.concatenate(tiles, axis=1)
+        out_ref[s, t] = o.reshape(height, cols, feats).astype(jnp.bfloat16)
+
+    for u in range(2):
+        for s in range(slabs):
+            for k in range(1, n_rows):
+                result(s, u, k).wait_recv()
+
+            def gather(t, carry, s=s):
+                placed(s, t)
+                return carry
+
+            lax.fori_loop(2 if u == 0 else 0, frames if u == 0 else 2, gather, 0)
 
     for s in range(1, n_rows):
         lat_copy(s).wait_send()
         for i in range(slabs):
-            result(i, s).wait_send()
+            for u in range(2):
+                result(i, u, s).wait_send()
     for k in range(n_rows - 1):
         for way in (1, -1):
             @pl.when(sends(k, way))
             def _():
                 hop(k, way).wait_send()
     for a in range(3):
+        give(a).wait_send()
         for s in range(1, half):
             direct(s, a).wait_send()
-        for s in range(half):
-            forward(s, a).wait_send()
+            forward(s, a, 0).wait_send()
+            if n_groups == 2:
+                swap(s, a).wait_send()
+                forward(s, a, 1).wait_send()
 
 
 def on_device(
@@ -339,12 +388,13 @@
         wt = jnp.pad(wt, ((0, cwp - cw), (0, 0)))
     vm = pl.BlockSpec(memory_space=pltpu.VMEM)
     sm = pl.BlockSpec(memory_space=pltpu.SMEM)
+    hbm = pl.BlockSpec(memory_space=pl.ANY)
     half = n_roll // 2
     dma = pltpu.SemaphoreType.DMA
     return pl.pallas_call(
-        functools.partial(kernel, n_roll, n_rows, cw),
+        functools.partial(kernel, lax.axis_size("groups"), n_roll, n_rows, cw),
         out_shape=jax.ShapeDtypeStruct((slabs, frames, height, cols, feats), jnp.bfloat16),
-        in_specs=[sm] * 3 + [vm] * 6,
+        in_specs=[sm] * 3 + [hbm, vm, hbm] + [vm] * 3,
         out_specs=vm,
         scratch_shapes=[
             pltpu.VMEM((n_roll, cwp, wt.shape[1]), jnp.bfloat16),
@@ -359,9 +409,10 @@
             pltpu.VMEM((slabs, n_rows, frames, cells, width), jnp.bfloat16),
             dma((3,)),
             dma((half, 3)), dma((half, 3)), dma((half, 3)), dma((half, 3)),
+            dma((2, half, 3)), dma((2, half, 3)),
             dma((n_rows,)), dma((n_rows,)),
             dma((2, n_rows)), dma((2, n_rows)),
-            dma((slabs, n_rows)), dma((slabs, n_rows)),
+            dma((slabs, 2, n_rows)), dma((slabs, 2, n_rows)),
         ],
         compiler_params=pltpu.CompilerParams(
             collective_id=0, has_side_effects=True, vmem_limit_bytes=67043328

time: 46.9 us -> 48 us (1.023)
  Pallas kernels: 43.2 us -> 44.3 us
    pallas_call x1, Pallas kernels: 43.2 us -> 44.3 us  [on_device(): pl.pallas_call(functools.partial(kernel, lax.axis_size('groups'), n_roll,...]
where the time goes in v3:
time: 48 us; the launch traced here: 47.8 us
  Pallas kernels  44.3 us (92%)
  local copies, waits for them, and re-layouts  2.53 us (5%)
  other arithmetic  0.93 us (2%)
    pallas_call x1, Pallas kernels, on_device(): pl.pallas_call(functools.partial(kernel, lax.axis_size('groups'), n_roll,...  44.3 us
    unnamed x1, local copies, waits for them, and re-layouts  1.78 us

profile of v3, /device:TPU:0, one launch (start us, length us, event | category | flops | bytes accessed | tf_op | source)
XLA Modules:
  0.0 47.8 jit_solution(9032243233370545021)
XLA Ops:
  0.0 0.9 %pad_maximum_fusion = bf16[2,5,8,8,16]{4,3,2,1,0:T(8,128)(2,1)S(1)} fusion(bf16[2,3,8,8,16]{4,3,2,1,0:T(8,128)(2,1)} %param.10, bf16[2,2,8,8,16]{4,3,2,1,0:T(8,128)(2,1)} %param.11), kind=kLoop, calls=%fused_computation | loop fusion | flops 10240 | bytes 40960 | tf_op jit(solution)/shard_map/concatenate | solution.py:384
  0.9 0.8 %reshape.3.lat_ref = bf16[2,5,8,128]{3,2,1,0:T(8,128)(2,1)} reshape(bf16[2,5,8,8,16]{4,3,2,1,0:T(8,128)(2,1)S(1)} %pad_maximum_fusion) | data formatting | bytes 40960 | tf_op jit(solution)/shard_map/reshape | solution.py:384
  1.7 44.3 %decode.1 = bf16[2,3,8,8,512]{4,3,2,1,0:T(8,128)(2,1)} custom-call(s32[2]{0:T(128)} %lengths_ref.1, s32[2]{0:T(128)} %starts_ref.1, s32[2]{0:T(128)} %plan_ref.1, bf16[32,13824]{1,0:T(8,128)(2,1)} %bitcast.5, bf16[2,5,8,128]{3,2,1,0:T(8,128)(2,1)} %reshape.3.lat_ref, bf16[2,2,8,8,512]{4,3,2,1,0:T(8,128)(2,1)} %feat_ref.1, bf16[432,512]{1,0:T(8,128)(2,1)} %ew_ref.1, ...), custom_call_target="tpu_custom_call" | custom-call | tf_op jit(solution)/shard_map/decode/pallas_call | solution.py:394
  46.0 1.8 %copy.12 = bf16[2,3,8,8,512]{4,3,2,1,0:T(8,128)(2,1)} copy(bf16[2,3,8,8,512]{4,3,2,1,0:T(8,128)(2,1)} %decode.1) | data formatting | bytes 786432

commit v4 on v3

--- a/solution.py
+++ b/solution.py
@@ -211,8 +211,8 @@
     lax.fori_loop(0, jobs // 3, entry, 0)
     pass_on(2)
     lax.fori_loop(jobs // 3, 2 * jobs // 3, entry, 0)
+    relay(1)
     pass_on(1)
-    relay(1)
     pass_swap(2)
     lax.fori_loop(2 * jobs // 3, jobs, entry, 0)
     pass_on(0)
@@ -247,10 +247,12 @@
             return carry
         lax.fori_loop(0, slabs, body, 0)
 
+    relay(2)
     arrive(2)
-    each(2, 0, frames)
-    relay(2)
-    pass_swap(0)
+    for s in range(slabs):
+        taps(2, s, 0, frames)
+        if s == 0:
+            pass_swap(0)
     arrive(1)
     each(1, 1, frames)
     arrive(0)

time: 48 us -> 46 us (0.958)
  Pallas kernels: 44.3 us -> 42.3 us
    pallas_call x1, Pallas kernels: 44.3 us -> 42.3 us  [on_device(): pl.pallas_call(functools.partial(kernel, lax.axis_size('groups'), n_roll,...]
where the time goes in v4:
time: 46 us; the launch traced here: 45.8 us
  Pallas kernels  42.3 us (92%)
  local copies, waits for them, and re-layouts  2.53 us (5%)
  other arithmetic  0.93 us (2%)
    pallas_call x1, Pallas kernels, on_device(): pl.pallas_call(functools.partial(kernel, lax.axis_size('groups'), n_roll,...  42.3 us
    unnamed x1, local copies, waits for them, and re-layouts  1.78 us
    concatenate x1, other arithmetic, on_device(): jnp.concatenate([prior_latents, latent_slabs], axis=1)  0.93 us

profile of v4, /device:TPU:0, one launch (start us, length us, event | category | flops | bytes accessed | tf_op | source)
XLA Modules:
  0.0 45.8 jit_solution(18079187482836141001)
XLA Ops:
  0.0 0.9 %pad_maximum_fusion = bf16[2,5,8,8,16]{4,3,2,1,0:T(8,128)(2,1)S(1)} fusion(bf16[2,3,8,8,16]{4,3,2,1,0:T(8,128)(2,1)} %param.10, bf16[2,2,8,8,16]{4,3,2,1,0:T(8,128)(2,1)} %param.11), kind=kLoop, calls=%fused_computation | loop fusion | flops 10240 | bytes 40960 | tf_op jit(solution)/shard_map/concatenate | solution.py:386
  0.9 0.8 %reshape.3.lat_ref = bf16[2,5,8,128]{3,2,1,0:T(8,128)(2,1)} reshape(bf16[2,5,8,8,16]{4,3,2,1,0:T(8,128)(2,1)S(1)} %pad_maximum_fusion) | data formatting | bytes 40960 | tf_op jit(solution)/shard_map/reshape | solution.py:386
  1.7 42.3 %decode.1 = bf16[2,3,8,8,512]{4,3,2,1,0:T(8,128)(2,1)} custom-call(s32[2]{0:T(128)} %lengths_ref.1, s32[2]{0:T(128)} %starts_ref.1, s32[2]{0:T(128)} %plan_ref.1, bf16[32,13824]{1,0:T(8,128)(2,1)} %bitcast.5, bf16[2,5,8,128]{3,2,1,0:T(8,128)(2,1)} %reshape.3.lat_ref, bf16[2,2,8,8,512]{4,3,2,1,0:T(8,128)(2,1)} %feat_ref.1, bf16[432,512]{1,0:T(8,128)(2,1)} %ew_ref.1, ...), custom_call_target="tpu_custom_call" | custom-call | tf_op jit(solution)/shard_map/decode/pallas_call | solution.py:396
  44.0 1.8 %copy.12 = bf16[2,3,8,8,512]{4,3,2,1,0:T(8,128)(2,1)} copy(bf16[2,3,8,8,512]{4,3,2,1,0:T(8,128)(2,1)} %decode.1) | data formatting | bytes 786432
